TPU v7x, 32 devices: a whole 2x2x4 slice. The times are simulated.
32 devices in a mesh: row: 8 (over y, x, core), col: 4 (over z).
Axes of the slice: x: 2, y: 2, z: 4, core: 2. Of those that a mesh axis runs over, the one named last changes fastest.
Arguments:
- matrix: float32 [9216, 9216], P('row', 'col'), as said below
Outputs:
- factored: float32 [9216, 9216], P('row', 'col')
Inputs may be any that keep to these rules, and one draw needn't show every extreme that they name: `matrix`: Off-diagonal entries are of order one; each diagonal entry lies between 4 * sqrt(256) and 8 * sqrt(256) times that.
All inputs are finite; a program needn't handle non-finite values.
Results may differ from a plain program's by a relative error of at most 0.0001.
Values sent between devices are 32-bit elements; how exact they have to be, the bound alone decides.
No kernel may reach another device: no remote copies, remote signals or barrier semaphores. Data moves between devices by JAX's collectives and lax.ppermute only.
A program may use at most 128 MiB of HBM per device.

v0:
```python
import jax
import jax.numpy as jnp
from jax import lax
from jax.sharding import PartitionSpec as P

B = 256
STEPS = 2


def from_root(array, axis, root):
    mine = lax.axis_index(axis) == root
    return lax.psum(jnp.where(mine, array, jnp.zeros_like(array)), axis)


def mult(left, right):
    return jnp.dot(left, right, precision=lax.Precision.HIGHEST, preferred_element_type=jnp.float32)


def spans(lead, width, extent):
    result = []
    for owner in range(lead // extent, (lead + width - 1) // extent + 1):
        low = max(lead, owner * extent) - owner * extent
        high = min(lead + width, (owner + 1) * extent) - owner * extent
        result.append((owner, low, high))
    return result


def cols_plain(tile, lead, cols):
    pieces = [
        from_root(tile[:, low:high], "col", owner) for owner, low, high in spans(lead, B, cols)
    ]
    return pieces[0]


def rows_joined(stacked, lead, rows):
    pieces = [
        from_root(stacked[low:high], "row", owner) for owner, low, high in spans(lead, B, rows)
    ]
    return jnp.concatenate(pieces, axis=0)


def inverse_of(block, eye):
    inverse = 1.0 / jnp.diagonal(block)
    first = inverse[:, None] * (2.0 * eye - block * inverse[None, :])
    return mult(first, 2.0 * eye - mult(block, first))


def on_device(matrix):
    rows, cols = matrix.shape
    row_ids = lax.axis_index("row") * rows + jnp.arange(rows, dtype=jnp.int32)[:, None]
    col_ids = lax.axis_index("col") * cols + jnp.arange(cols, dtype=jnp.int32)[None, :]
    eye = jnp.eye(B, dtype=jnp.float32)
    tile = matrix
    for step in range(STEPS):
        lead = step * B
        panel = cols_plain(tile, lead, cols)
        joined = rows_joined(jnp.concatenate([tile, panel], axis=1), lead, rows)
        upper = joined[:, :cols]
        lower = mult(panel, inverse_of(joined[:, cols:], eye))
        update = mult(lower, upper)
        picked = jnp.take(lower, jnp.clip(col_ids[0] - lead, 0, B - 1), axis=1)
        below = row_ids >= lead + B
        right = col_ids >= lead + B
        inside = (col_ids >= lead) & (col_ids < lead + B)
        tile = jnp.where(below & right, tile - update, jnp.where(below & inside, picked, tile))
    return tile


def solution(mesh):
    return jax.shard_map(
        on_device,
        mesh=mesh,
        in_specs=(P("row", "col"),),
        out_specs=P("row", "col"),
        check_vma=False,
    )
```

profile of v0, /device:TPU:0, one launch (start us, length us, event | category | flops | bytes accessed | tf_op | source)
XLA Modules:
  0.0 363.7 jit_solution(15044023038616365987)
XLA Ops:
  6.5 0.0 all-reduce.5.cloned.1.call-start
  6.5 2.4 slice_select_fusion.1
  8.9 0.0 all-reduce.5.cloned.1.call-update
  8.9 0.0 all-reduce.7.cloned.1.call-start
  9.0 59.5 %all-reduce.5.cloned.1.call-done = f32[1152,256]{1,0:T(8,128)} async-done(((f32[1152,256]{1,0:T(8,128)}), f32[1152,256]{1,0:T(8,128)}) %all-reduce.5.cloned.1.call-update) | async-done | bytes 1179664 | tf_op jit(solution)/shard_map/psum | solution.py:12
  68.5 3.6 fusion.3
  72.0 0.0 all-reduce.7.cloned.1.call-update
  72.1 0.0 all-reduce.9.cloned.1.call-start
  72.1 0.6 fusion.37
  72.7 0.6 compare_and_fusion.1
  73.3 0.6 fusion.33
  74.0 62.3 %all-reduce.7.cloned.1.call-done = f32[256,2560]{1,0:T(8,128)} async-done(((f32[256,2560]{1,0:T(8,128)}), f32[256,2560]{1,0:T(8,128)}) %all-reduce.7.cloned.1.call-update) | async-done | bytes 2621456 | tf_op jit(solution)/shard_map/psum | solution.py:12
  136.3 1.0 slice.40
  137.3 2.3 gather_fusion
  139.6 1.5 convolution_subtract_fusion.3
  141.1 1.4 fusion.11
  142.5 0.0 copy-done.1
  142.5 1.1 fusion.51
  143.6 0.4 copy.6
  144.0 8.8 %gather_fusion.2 = f32[2304,1152]{1,0:T(8,128)} fusion(f32[1152,256]{0,1:T(8,128)S(1)} %copy.6, s32[3072]{0:T(1024)S(1)} %pad_clamp_fusion.1), kind=kCustom, calls=%fused_computation.clone | custom fusion | bytes 21242880 | tf_op jit(solution)/shard_map/jit(_take)/gather | solution.py:61
  152.8 12.7 %copy.7 = f32[2304,1152]{0,1:T(8,128)} copy(f32[2304,1152]{1,0:T(8,128)} %gather_fusion.2) | data formatting | bytes 21233664 | tf_op jit(solution)/shard_map/jit(_take)/gather | solution.py:61
  165.5 0.0 copy-done.3
  165.5 0.0 copy-done.6
  165.5 0.0 copy-done.7
  165.5 0.0 copy-done.9
  165.5 16.1 %fusion.1 = f32[1152,2304]{1,0:T(8,128)S(1)} fusion(f32[1152,2304]{1,0:T(8,128)} %param.3, f32[1152,256]{1,0:T(8,128)S(1)} %fusion.51, f32[2304,1152]{0,1:T(8,128)} %copy.7, pred[2304]{0:T(1024)(128)(4,1)S(1)} %copy-done.3, pred[2304]{0:T(1024)(128)(4,1)S(1)} %copy-done.7, pred[2304]{0:T(1024)(128)(4,1)S(1)} %copy-done.6, pred[1152]{0:T(1024)(128)(4,1)S(1)} %copy-done.9, ...), kind=kOutput, calls=%fused_computation.7 | convolution fusion | flops 8169652224 | bytes 35397504 | tf_op jit(solution)/shard_map/dot_general | solution.py:16
  181.6 0.0 copy-start
  181.6 4.1 %copy-done = f32[1152,2304]{1,0:T(8,128)} copy-done((f32[1152,2304]{1,0:T(8,128)}, f32[1152,2304]{1,0:T(8,128)S(1)}, u32[]{:S(2)}) %copy-start) | copy-done | bytes 10616856
  185.7 1.1 slice_select_fusion
  186.8 0.0 all-reduce.9.cloned.1.call-update
  186.9 0.2 all-reduce.11.cloned.1.call-start
  187.1 55.4 %all-reduce.9.cloned.1.call-done = f32[1152,256]{1,0:T(8,128)} async-done(((f32[1152,256]{1,0:T(8,128)}), f32[1152,256]{1,0:T(8,128)}) %all-reduce.9.cloned.1.call-update) | async-done | bytes 1179664 | tf_op jit(solution)/shard_map/psum | solution.py:12
  242.5 3.6 fusion.2
  246.2 0.0 all-reduce.11.cloned.1.call-update
  246.2 0.6 fusion.38
  246.8 0.6 fusion.34
  247.4 63.0 %all-reduce.11.cloned.1.call-done = f32[256,2560]{1,0:T(8,128)} async-done(((f32[256,2560]{1,0:T(8,128)}), f32[256,2560]{1,0:T(8,128)}) %all-reduce.11.cloned.1.call-update) | async-done | bytes 2621456 | tf_op jit(solution)/shard_map/psum | solution.py:12
  310.4 1.0 slice.43
  311.4 2.3 gather_fusion.1
  313.7 1.5 convolution_subtract_fusion.2
  315.2 1.4 fusion.8
  316.6 1.1 fusion.52
  317.7 0.4 copy.8
  318.1 8.9 %gather_fusion.3 = f32[2304,1152]{1,0:T(8,128)} fusion(f32[1152,256]{0,1:T(8,128)S(1)} %copy.8, s32[3072]{0:T(1024)S(1)} %pad_clamp_fusion), kind=kCustom, calls=%fused_computation.1.clone | custom fusion | bytes 21242880 | tf_op jit(solution)/shard_map/jit(_take)/gather | solution.py:61
  327.0 12.7 %copy.9 = f32[2304,1152]{0,1:T(8,128)} copy(f32[2304,1152]{1,0:T(8,128)} %gather_fusion.3) | data formatting | bytes 21233664 | tf_op jit(solution)/shard_map/jit(_take)/gather | solution.py:61
  339.7 0.0 copy-done.4
  339.7 0.0 copy-done.8
  339.7 17.5 %fusion = f32[1152,2304]{1,0:T(8,128)} fusion(f32[1152,2304]{1,0:T(8,128)} %copy-done, f32[1152,256]{1,0:T(8,128)S(1)} %fusion.52, f32[2304,1152]{0,1:T(8,128)} %copy.9, pred[2304]{0:T(1024)(128)(4,1)S(1)} %compare_and_fusion, pred[2304]{0:T(1024)(128)(4,1)S(1)} %copy-done.5, pred[2304]{0:T(1024)(128)(4,1)S(1)} %copy-done.4, ...), kind=kOutput, calls=%fused_computation.5 | convolution fusion | flops 8169652224 | bytes 35397504 | tf_op jit(solution)/shard_map/dot_general | solution.py:16
  (19 shorter events, 0.1 us)
Async XLA Ops:
  6.5 61.9 %all-reduce.5.cloned.1.call-start = ((), (), s32[]{:S(2)}) async-start(), calls=%async_computation | async-start | bytes 2359296 | tf_op jit(solution)/shard_map/psum | solution.py:12
  8.9 127.4 %all-reduce.7.cloned.1.call-start = ((), (), s32[]{:S(2)}) async-start(), calls=%async_computation.1 | async-start | bytes 5242880 | tf_op jit(solution)/shard_map/psum | solution.py:12
  72.0 70.5 %copy-start.1 = (f32[1152,256]{1,0:T(8,128)S(1)}, f32[1152,256]{1,0:T(8,128)}, u32[]{:S(2)}) copy-start(f32[1152,256]{1,0:T(8,128)} %all-reduce.5.cloned.1.call-done) | copy-start | bytes 3538948
  72.1 170.5 %all-reduce.9.cloned.1.call-start = ((), (), s32[]{:S(2)}) async-start(), calls=%async_computation.2 | async-start | bytes 2359296 | tf_op jit(solution)/shard_map/psum | solution.py:12
  152.8 12.7 %copy-start.3 = (pred[2304]{0:T(1024)(128)(4,1)S(1)}, pred[2304]{0:T(1024)(128)(4,1)}, u32[]{:S(2)}) copy-start(pred[2304]{0:T(1024)(128)(4,1)} %compare_and_fusion.1) | copy-start | bytes 6916
  152.8 12.7 %copy-start.6 = (pred[2304]{0:T(1024)(128)(4,1)S(1)}, pred[2304]{0:T(1024)(128)(4,1)}, u32[]{:S(2)}) copy-start(pred[2304]{0:T(1024)(128)(4,1)} %get-tuple-element.6) | copy-start | bytes 6916
  152.8 12.7 %copy-start.7 = (pred[2304]{0:T(1024)(128)(4,1)S(1)}, pred[2304]{0:T(1024)(128)(4,1)}, u32[]{:S(2)}) copy-start(pred[2304]{0:T(1024)(128)(4,1)} %get-tuple-element.7) | copy-start | bytes 6916
  152.8 12.7 %copy-start.9 = (pred[1152]{0:T(1024)(128)(4,1)S(1)}, pred[1152]{0:T(1024)(128)(4,1)}, u32[]{:S(2)}) copy-start(pred[1152]{0:T(1024)(128)(4,1)} %fusion.37) | copy-start | bytes 3460
  181.6 4.1 %copy-start = (f32[1152,2304]{1,0:T(8,128)}, f32[1152,2304]{1,0:T(8,128)S(1)}, u32[]{:S(2)}) copy-start(f32[1152,2304]{1,0:T(8,128)S(1)} %fusion.1) | copy-start | bytes 31850500
  186.9 123.5 %all-reduce.11.cloned.1.call-start = ((), (), s32[]{:S(2)}) async-start(), calls=%async_computation.3 | async-start | bytes 5242880 | tf_op jit(solution)/shard_map/psum | solution.py:12
  246.2 70.5 %copy-start.2 = (f32[1152,256]{1,0:T(8,128)S(1)}, f32[1152,256]{1,0:T(8,128)}, u32[]{:S(2)}) copy-start(f32[1152,256]{1,0:T(8,128)} %all-reduce.9.cloned.1.call-done) | copy-start | bytes 3538948
  327.0 12.7 %copy-start.4 = (pred[2304]{0:T(1024)(128)(4,1)S(1)}, pred[2304]{0:T(1024)(128)(4,1)}, u32[]{:S(2)}) copy-start(pred[2304]{0:T(1024)(128)(4,1)} %get-tuple-element.8) | copy-start | bytes 6916
  327.0 12.7 %copy-start.5 = (pred[2304]{0:T(1024)(128)(4,1)S(1)}, pred[2304]{0:T(1024)(128)(4,1)}, u32[]{:S(2)}) copy-start(pred[2304]{0:T(1024)(128)(4,1)} %get-tuple-element.9) | copy-start | bytes 6916
  327.0 12.7 %copy-start.8 = (pred[1152]{0:T(1024)(128)(4,1)S(1)}, pred[1152]{0:T(1024)(128)(4,1)}, u32[]{:S(2)}) copy-start(pred[1152]{0:T(1024)(128)(4,1)} %fusion.38) | copy-start | bytes 3460
Sparse Core Ops, SparseCore 0:
  9.7 58.6 all-reduce.4
  72.2 64.0 all-reduce.6
  187.0 55.5 all-reduce.8
  246.3 64.0 all-reduce.10
where the time goes:
time: 365 us; the launch traced here: 364 us
  waiting for transfers between devices  240 us (66%)
  local copies, waits for them, and re-layouts  54.6 us (15%)
  matrix products  41.4 us (11%)
  other arithmetic  13.7 us (4%)
  between operations  13.3 us (4%)
    psum x4, waiting for transfers between devices, from_root(): return lax.psum(jnp.where(mine, array, jnp.zeros_like(array)), axis)  240 us
    gather x4, local copies, waits for them, and re-layouts, on_device(): picked = jnp.take(lower, jnp.clip(col_ids[0] - lead, 0, B - 1), axis=1)  43.1 us
    dot_general x8, matrix products, mult(): jnp.dot(left, right, precision=lax.Precision.HIGHEST, preferred_element_t...  41.4 us
    select_n x4, other arithmetic, from_root(): return lax.psum(jnp.where(mine, array, jnp.zeros_like(array)), axis)  10.7 us
  transfers between devices with their start and end apart: 4, of which 4 were waited for; matrix products, arithmetic and copies ran while one was open for 1% of the time, Pallas kernels for 0%

commit v1 on v0

--- a/solution.py
+++ b/solution.py
@@ -7,9 +7,15 @@
 STEPS = 2
 
 
+def add_all(value, name):
+    parts = lax.all_gather(value, name, axis=0, tiled=False)
+    total = parts.sum(axis=0)
+    return total
+
+
 def from_root(array, axis, root):
     mine = lax.axis_index(axis) == root
-    return lax.psum(jnp.where(mine, array, jnp.zeros_like(array)), axis)
+    return add_all(jnp.where(mine, array, jnp.zeros_like(array)), axis)
 
 
 def mult(left, right):

time: 365 us -> 539 us (1.48)
  waiting for transfers between devices: 240 us -> 393 us
  other arithmetic: 13.7 us -> 34.5 us
    all_gather x0 -> x4, waiting for transfers between devices: none -> 393 us  [add_all(): parts = lax.all_gather(value, name, axis=0, tiled=False)]
    psum x4 -> x0, waiting for transfers between devices: 240 us -> none  [from_root(): return lax.psum(jnp.where(mine, array, jnp.zeros_like(array)), axis)]
    reduce_sum x0 -> x4, other arithmetic: none -> 23 us  [add_all(): total = parts.sum(axis=0)]
  transfers between devices with their start and end apart: 4 -> 4, of which waited for: 4 -> 4; matrix products, arithmetic and copies ran while one was open for 1% -> 0% of each run, Pallas kernels for 0% -> 0%
where the time goes in v1:
time: 539 us; the launch traced here: 538 us
  waiting for transfers between devices  393 us (73%)
  local copies, waits for them, and re-layouts  55.5 us (10%)
  matrix products  41.1 us (8%)
  other arithmetic  34.5 us (6%)
  between operations  13.4 us (2%)
    all_gather x4, waiting for transfers between devices, add_all(): parts = lax.all_gather(value, name, axis=0, tiled=False)  393 us
    gather x4, local copies, waits for them, and re-layouts, on_device(): picked = jnp.take(lower, jnp.clip(col_ids[0] - lead, 0, B - 1), axis=1)  43.4 us
    dot_general x8, matrix products, mult(): jnp.dot(left, right, precision=lax.Precision.HIGHEST, preferred_element_t...  41.1 us
    reduce_sum x4, other arithmetic, add_all(): total = parts.sum(axis=0)  23 us
    select_n x4, other arithmetic, from_root(): return add_all(jnp.where(mine, array, jnp.zeros_like(array)), axis)  11.4 us
  transfers between devices with their start and end apart: 4, of which 4 were waited for; matrix products, arithmetic and copies ran while one was open for 0% of the time, Pallas kernels for 0%

profile of v1, /device:TPU:0, one launch (start us, length us, event | category | flops | bytes accessed | tf_op | source)
XLA Modules:
  0.0 538.3 jit_solution(17056994639685661695)
XLA Ops:
  6.5 0.0 all-gather.9.cloned.1.call-start
  6.5 2.4 slice_select_fusion.1
  8.9 0.0 all-gather.9.cloned.1.call-update
  8.9 0.0 all-gather.11.cloned.1.call-start
  9.0 92.2 %all-gather.9.cloned.1.call-done = f32[4608,256]{1,0:T(8,128)} async-done(((f32[1152,256]{1,0:T(8,128)}), f32[4608,256]{1,0:T(8,128)}) %all-gather.9.cloned.1.call-update) | async-done | bytes 4718608 | tf_op jit(solution)/shard_map/all_gather | solution.py:11
  101.2 2.8 reduce_sum.36
  104.0 0.0 copy-start.5
  104.0 3.9 fusion.3
  108.0 0.0 copy-done.5
  108.0 0.0 all-gather.11.cloned.1.call-update
  108.0 0.0 all-gather.13.cloned.1.call-start
  108.2 105.9 %all-gather.11.cloned.1.call-done = f32[2048,2560]{1,0:T(8,128)} async-done(((f32[256,2560]{1,0:T(8,128)}), f32[2048,2560]{1,0:T(8,128)}) %all-gather.11.cloned.1.call-update) | async-done | bytes 20971536 | tf_op jit(solution)/shard_map/all_gather | solution.py:11
  214.0 8.7 %reduce_sum.37 = f32[256,2560]{1,0:T(8,128)S(1)} reduce(f32[8,256,2560]{2,1,0:T(8,128)} %bitcast.23, f32[]{:T(128)} %constant.12.clone.1), dimensions={0}, to_apply=%region_1.2 | reduce | flops 4587520 | bytes 23592964 | tf_op jit(solution)/shard_map/reduce_sum | solution.py:12
  222.7 0.0 copy-start.3
  222.7 2.3 gather_fusion
  225.1 0.5 convolution_subtract_fusion.3
  225.6 0.4 fusion.11
  226.0 0.0 copy-done.3
  226.0 3.4 fusion.51
  229.4 1.6 copy.6
  231.0 8.8 %gather_fusion.2 = f32[2304,1152]{1,0:T(8,128)} fusion(f32[1152,256]{0,1:T(8,128)S(1)} %copy.6, s32[3072]{0:T(1024)S(1)} %pad_clamp_fusion.1), kind=kCustom, calls=%fused_computation.clone | custom fusion | bytes 21242880 | tf_op jit(solution)/shard_map/jit(_take)/gather | solution.py:67
  239.8 12.8 %copy.7 = f32[2304,1152]{0,1:T(8,128)} copy(f32[2304,1152]{1,0:T(8,128)} %gather_fusion.2) | data formatting | bytes 21233664 | tf_op jit(solution)/shard_map/jit(_take)/gather | solution.py:67
  252.6 0.0 copy-done.4
  252.6 15.2 %fusion.1 = f32[1152,2304]{1,0:T(8,128)S(1)} fusion(f32[1152,2304]{1,0:T(8,128)} %param.3, f32[1152,256]{1,0:T(8,128)} %fusion.51, f32[2304,1152]{0,1:T(8,128)} %copy.7, pred[2304]{0:T(1024)(128)(4,1)S(1)} %compare_and_fusion.1, pred[2304]{0:T(1024)(128)(4,1)S(1)} %get-tuple-element.7, pred[2304]{0:T(1024)(128)(4,1)S(1)} %get-tuple-element.6, ...), kind=kOutput, calls=%fused_computation.7 | convolution fusion | flops 8169652224 | bytes 35400704 | tf_op jit(solution)/shard_map/dot_general | solution.py:22
  267.9 0.0 copy-start
  267.9 4.1 copy-done
  272.0 1.1 slice_select_fusion
  273.2 0.0 all-gather.13.cloned.1.call-update
  273.2 0.2 all-gather.15.cloned.1.call-start
  273.4 89.3 %all-gather.13.cloned.1.call-done = f32[4608,256]{1,0:T(8,128)} async-done(((f32[1152,256]{1,0:T(8,128)}), f32[4608,256]{1,0:T(8,128)}) %all-gather.13.cloned.1.call-update) | async-done | bytes 4718608 | tf_op jit(solution)/shard_map/all_gather | solution.py:11
  362.7 2.8 reduce_sum.38
  365.6 0.0 copy-start.6
  365.6 4.0 fusion.2
  369.5 0.0 copy-done.6
  369.5 0.0 all-gather.15.cloned.1.call-update
  369.7 105.9 %all-gather.15.cloned.1.call-done = f32[2048,2560]{1,0:T(8,128)} async-done(((f32[256,2560]{1,0:T(8,128)}), f32[2048,2560]{1,0:T(8,128)}) %all-gather.15.cloned.1.call-update) | async-done | bytes 20971536 | tf_op jit(solution)/shard_map/all_gather | solution.py:11
  475.6 8.7 %reduce_sum.39 = f32[256,2560]{1,0:T(8,128)S(1)} reduce(f32[8,256,2560]{2,1,0:T(8,128)} %bitcast.24, f32[]{:T(128)} %constant.12.clone.1), dimensions={0}, to_apply=%region_3.5 | reduce | flops 4587520 | bytes 23592964 | tf_op jit(solution)/shard_map/reduce_sum | solution.py:12
  484.3 0.0 copy-start.1
  484.3 2.3 gather_fusion.1
  486.7 0.5 convolution_subtract_fusion.2
  487.1 0.4 fusion.8
  487.6 0.0 copy-done.1
  487.6 3.5 fusion.52
  491.0 1.6 copy.8
  492.7 8.9 %gather_fusion.3 = f32[2304,1152]{1,0:T(8,128)} fusion(f32[1152,256]{0,1:T(8,128)S(1)} %copy.8, s32[3072]{0:T(1024)S(1)} %pad_clamp_fusion), kind=kCustom, calls=%fused_computation.1.clone | custom fusion | bytes 21242880 | tf_op jit(solution)/shard_map/jit(_take)/gather | solution.py:67
  501.6 12.8 %copy.9 = f32[2304,1152]{0,1:T(8,128)} copy(f32[2304,1152]{1,0:T(8,128)} %gather_fusion.3) | data formatting | bytes 21233664 | tf_op jit(solution)/shard_map/jit(_take)/gather | solution.py:67
  514.4 0.0 copy-done.2
  514.4 17.3 %fusion = f32[1152,2304]{1,0:T(8,128)} fusion(f32[1152,2304]{1,0:T(8,128)} %copy-done, f32[1152,256]{1,0:T(8,128)} %fusion.52, f32[2304,1152]{0,1:T(8,128)} %copy.9, pred[2304]{0:T(1024)(128)(4,1)S(1)} %compare_and_fusion, pred[2304]{0:T(1024)(128)(4,1)S(1)} %get-tuple-element.9, pred[2304]{0:T(1024)(128)(4,1)S(1)} %get-tuple-element.8, ...), kind=kOutput, calls=%fused_computation.5 | convolution fusion | flops 8169652224 | bytes 35400704 | tf_op jit(solution)/shard_map/dot_general | solution.py:22
  (17 shorter events, 0.2 us)
Async XLA Ops:
  6.5 94.7 %all-gather.9.cloned.1.call-start = ((), (), s32[]{:S(2)}) async-start(), calls=%async_computation | async-start | bytes 5898240 | tf_op jit(solution)/shard_map/all_gather | solution.py:11
  8.9 205.1 %all-gather.11.cloned.1.call-start = ((), (), s32[]{:S(2)}) async-start(), calls=%async_computation.1 | async-start | bytes 23592960 | tf_op jit(solution)/shard_map/all_gather | solution.py:11
  104.0 3.9 copy-start.5
  108.0 254.7 %all-gather.13.cloned.1.call-start = ((), (), s32[]{:S(2)}) async-start(), calls=%async_computation.2 | async-start | bytes 5898240 | tf_op jit(solution)/shard_map/all_gather | solution.py:11
  222.7 3.3 copy-start.3
  239.8 12.8 %copy-start.4 = (f32[256,2560]{1,0:T(8,128)S(1)}, f32[256,2560]{1,0:T(8,128)}, u32[]{:S(2)}) copy-start(f32[256,2560]{1,0:T(8,128)} %copy-done.3) | copy-start | bytes 7864324
  267.9 4.1 copy-start
  273.2 202.4 %all-gather.15.cloned.1.call-start = ((), (), s32[]{:S(2)}) async-start(), calls=%async_computation.3 | async-start | bytes 23592960 | tf_op jit(solution)/shard_map/all_gather | solution.py:11
  365.6 4.0 copy-start.6
  484.3 3.3 copy-start.1
  501.6 12.8 %copy-start.2 = (f32[256,2560]{1,0:T(8,128)S(1)}, f32[256,2560]{1,0:T(8,128)}, u32[]{:S(2)}) copy-start(f32[256,2560]{1,0:T(8,128)} %copy-done.1) | copy-start | bytes 7864324
Sparse Core Ops, SparseCore 0:
  9.0 92.0 all-gather.8
  108.1 105.8 all-gather.10
  273.3 89.3 all-gather.12
  369.7 105.8 all-gather.14
